TPU v7x, 128 devices: a whole 4x4x4 slice. The times are simulated.
128 devices in a mesh: row: 16 (over y, z_hi, core), col: 8 (over x, z_lo).
Axes of the slice: x: 4, y: 4, z: 4 (z_hi: 2, z_lo: 2; z = z_hi * 2 + z_lo), core: 2. Of those that a mesh axis runs over, the one named last changes fastest.
Arguments:
- aligned_family_embedding: bfloat16 [512, 768, 256], P('row', 'col'), may hold values from -24 to 24
- aligned_slot_available: int32 [512, 768], P('row', 'col'), may hold values from 0 to 1, as said below
- chain_site_available: int32 [768], replicated, may hold values 0 or 1
- duo_embedding: float32 [768, 768, 128], P('row', 'col'), may hold values from -1.2 to 1.2
- averaging_layernorm_stretch: float32 [256], replicated, may hold values from 0.1 to 1.9
- lineup_layernorm_stretch: float32 [256], replicated, may hold values from 0.1 to 1.9
- duo_layernorm_stretch: float32 [128], replicated, may hold values from 0.1 to 1.9
- lefthand_linear_kernel: bfloat16 [256, 32], replicated, may hold values from -0.375 to 0.375
- righthand_linear_kernel: bfloat16 [256, 32], replicated, may hold values from -0.375 to 0.375
- kronecker_linear_kernel: bfloat16 [1024, 128], replicated, may hold values from -0.1875 to 0.1875
- duo_logit_kernel: bfloat16 [128, 8], replicated, may hold values from -0.75 to 0.75
- asker_lookup_sigmoid_kernel: bfloat16 [256, 1024], replicated, may hold values from -8 to 8
- closing_linear_kernel: bfloat16 [256, 256], replicated, may hold values from -0.375 to 0.375
Outputs:
- refreshed_family_embedding: bfloat16 [512, 768, 256], P('row', 'col')
- duo_after_averaging: float32 [768, 768, 128], P('row', 'col')
Inputs may be any that keep to these rules, and one draw needn't show every extreme that they name: `aligned_slot_available`: 0 or 1; sequence 0 is present at every residue.
All inputs are finite; a program needn't handle non-finite values.
Results may differ from a plain program's by a relative error of at most 0.0052.
Values may be sent and summed in bfloat16 or wider, within the bound.
A program may use at most 192 MiB of HBM per device.

v0:
```python
import jax
import jax.numpy as jnp
from jax import lax
from jax.sharding import PartitionSpec as P

EPSILON = 1e-05
CONTRACT_FIRST = (((0,), (0,)), ((), ()))


def laid_out(pieces, dim):
    lengths = list(pieces.shape[1:])
    lengths[dim] *= pieces.shape[0]
    return jnp.moveaxis(pieces, 0, dim).reshape(lengths)


def one_gather(arrays, axis, dims):
    line = jnp.concatenate([a.reshape(-1) for a in arrays])
    lines, at, outs = (lax.all_gather(line, axis), 0, [])
    for a, dim in zip(arrays, dims):
        pieces = lines[:, at : at + a.size].reshape(-1, *a.shape)
        outs.append(laid_out(pieces, dim))
        at += a.size
    return tuple(outs)


def in_one_piece(arrays, axis, dim, along):
    ends, at = ([], 0)
    for a in arrays[:-1]:
        at += a.shape[along]
        ends.append(at)
    both = jnp.concatenate(arrays, axis=along)
    return tuple(jnp.split(lax.all_gather(both, axis, axis=dim, tiled=True), ends, axis=along))


def sent_to_all(x, axis):
    copies = jnp.broadcast_to(x, (lax.axis_size(axis), *x.shape))
    return lax.all_to_all(copies, axis, split_axis=0, concat_axis=0, tiled=True)


def gather_directly(x, axis, dim):
    return laid_out(sent_to_all(x, axis), dim)


def sent_together(arrays, axis, split_dim, concat_dim, along):
    columns = [a.reshape(*a.shape[:along], -1) for a in arrays]
    both = jnp.concatenate(columns, axis=along)
    whole, at, outs = (
        lax.all_to_all(both, axis, split_axis=split_dim, concat_axis=concat_dim, tiled=True),
        0,
        [],
    )
    for a, column in zip(arrays, columns):
        section = whole[..., at : at + column.shape[along]]
        outs.append(section.reshape(*section.shape[:along], *a.shape[along:]))
        at += column.shape[along]
    return tuple(outs)


def standardize_features(values):
    average = jnp.mean(values, axis=-1, keepdims=True)
    centred = values - average
    variance = jnp.mean(centred * centred, axis=-1, keepdims=True)
    return centred * lax.rsqrt(variance + EPSILON)


def project_rows(inputs, weight, availability_real):
    projected = jnp.einsum("src,ca->sra", inputs, weight, preferred_element_type=jnp.float32)
    return (projected * availability_real[:, :, None]).astype(jnp.bfloat16)


def attend(queries, gate_pre, keys_all, values_all, key_mask, bias_rows, head_count):
    homolog_number, query_count, inner_width = queries.shape
    key_count = keys_all.shape[1]
    head_dim = inner_width // head_count
    block_rows = 1
    while (
        block_rows < homolog_number
        and block_rows * query_count < 512
        and (homolog_number % (2 * block_rows) == 0)
    ):
        block_rows = 2 * block_rows
    groups = homolog_number // block_rows
    score_scale = head_dim ** (-0.5)
    bias_float = bias_rows.astype(jnp.float32)

    def one_block(group_members):
        block_query, block_gate, block_key, block_value, block_mask = group_members
        query_heads = block_query.reshape(block_rows, query_count, head_count, head_dim)
        key_heads = block_key.reshape(block_rows, key_count, head_count, head_dim)
        value_heads = block_value.reshape(block_rows, key_count, head_count, head_dim)
        scores = jnp.einsum(
            "bqhd,bkhd->bhqk", query_heads, key_heads, preferred_element_type=jnp.float32
        )
        scores = (
            scores * score_scale
            + bias_float[None]
            + 1000000000.0 * (block_mask.astype(jnp.float32)[:, None, None, :] - 1.0)
        )
        highest = jnp.max(scores, axis=-1, keepdims=True)
        exponent = jnp.exp(scores - highest)
        weights = (exponent / jnp.sum(exponent, axis=-1, keepdims=True)).astype(jnp.bfloat16)
        mixed_rows = jnp.einsum(
            "bhqk,bkhd->bqhd", weights, value_heads, preferred_element_type=jnp.float32
        )
        mixed_rows = mixed_rows.reshape(block_rows, query_count, inner_width)
        return (mixed_rows * jax.nn.sigmoid(block_gate.astype(jnp.float32))).astype(jnp.bfloat16)

    def grouped(array):
        return array.reshape((groups, block_rows) + array.shape[1:])

    gated_row_output = lax.map(
        one_block,
        (
            grouped(queries),
            grouped(gate_pre),
            grouped(keys_all),
            grouped(values_all),
            grouped(key_mask),
        ),
    )
    return gated_row_output.reshape(homolog_number, query_count, inner_width)


def shards(
    aligned_family_embedding,
    aligned_slot_available,
    chain_site_available,
    duo_embedding,
    averaging_layernorm_stretch,
    lineup_layernorm_stretch,
    duo_layernorm_stretch,
    lefthand_linear_kernel,
    righthand_linear_kernel,
    kronecker_linear_kernel,
    duo_logit_kernel,
    asker_lookup_sigmoid_kernel,
    closing_linear_kernel,
):
    homolog_number, amino_position_number, discarded_carry = aligned_family_embedding.shape
    res_rows = duo_embedding.shape[0]
    opm_width = lefthand_linear_kernel.shape[1]
    head_count = duo_logit_kernel.shape[1]
    inner_width = closing_linear_kernel.shape[0]
    row_index = lax.axis_index("row")
    col_index = lax.axis_index("col")
    standardized_features = standardize_features(aligned_family_embedding.astype(jnp.float32))
    availability_real = aligned_slot_available.astype(jnp.float32)
    shrunk_availability = aligned_slot_available.astype(jnp.bfloat16)
    opm_input = (standardized_features * averaging_layernorm_stretch).astype(jnp.bfloat16)
    left_flat = project_rows(opm_input, lefthand_linear_kernel, availability_real).reshape(
        homolog_number, amino_position_number * opm_width
    )
    right_flat = project_rows(opm_input, righthand_linear_kernel, availability_real).reshape(
        homolog_number, amino_position_number * opm_width
    )
    left_wide, mask_wide = one_gather((left_flat, shrunk_availability), "col", (1, 1))
    left_block, left_mask = (
        lax.all_to_all(left_wide, "row", split_axis=1, concat_axis=0, tiled=True),
        lax.all_to_all(mask_wide, "row", split_axis=1, concat_axis=0, tiled=True),
    )
    right_all, mask_all = in_one_piece((right_flat, shrunk_availability), "row", 0, 1)
    outer_sum = lax.dot_general(
        left_block, right_all, CONTRACT_FIRST, preferred_element_type=jnp.float32
    )
    counts = lax.dot_general(
        left_mask, mask_all, CONTRACT_FIRST, preferred_element_type=jnp.float32
    )
    outer_narrow = outer_sum.astype(jnp.bfloat16).reshape(
        res_rows, opm_width, amino_position_number, opm_width
    )
    mixing = kronecker_linear_kernel.reshape(opm_width, opm_width, kronecker_linear_kernel.shape[1])
    update = jnp.einsum("iajb,abk->ijk", outer_narrow, mixing, preferred_element_type=jnp.float32)
    residue_float = chain_site_available.astype(jnp.float32)
    residue_rows = lax.dynamic_slice_in_dim(residue_float, row_index * res_rows, res_rows)
    residue_cols = lax.dynamic_slice_in_dim(
        residue_float, col_index * amino_position_number, amino_position_number
    )
    update = (
        update
        / (counts + 0.001)[:, :, None]
        * (residue_rows[:, None] * residue_cols[None, :])[:, :, None]
    )
    duo_after_averaging = duo_embedding + update
    pair_input = (standardize_features(duo_after_averaging) * duo_layernorm_stretch).astype(
        jnp.bfloat16
    )
    bias_tile = jnp.einsum(
        "ijc,ch->hij", pair_input, duo_logit_kernel, preferred_element_type=jnp.float32
    ).astype(jnp.bfloat16)
    bias_cols = gather_directly(bias_tile, "col", 2)
    exponential_probabilities = (standardized_features * lineup_layernorm_stretch).astype(
        jnp.bfloat16
    )
    rows_input, rows_mask = sent_together(
        (exponential_probabilities, shrunk_availability), "col", 0, 1, 2
    )
    bias_whole = lax.all_gather(bias_cols, "row", axis=1, tiled=True)
    projected = jnp.einsum(
        "src,cd->srd", rows_input, asker_lookup_sigmoid_kernel, preferred_element_type=jnp.float32
    ).astype(jnp.bfloat16)
    gated_whole = attend(
        projected[..., :inner_width],
        projected[..., 3 * inner_width :],
        projected[..., inner_width : 2 * inner_width],
        projected[..., 2 * inner_width : 3 * inner_width],
        rows_mask,
        bias_whole,
        head_count,
    )
    gated_local = lax.all_to_all(gated_whole, "col", split_axis=1, concat_axis=0, tiled=True)
    summed_increment = jnp.einsum(
        "sqd,dc->sqc", gated_local, closing_linear_kernel, preferred_element_type=jnp.float32
    )
    refreshed_family_embedding = (
        aligned_family_embedding.astype(jnp.float32) + summed_increment
    ).astype(jnp.bfloat16)
    return (refreshed_family_embedding, duo_after_averaging)


def solution(mesh):
    placed = (
        P("row", "col", None),
        P("row", "col"),
        P(),
        P("row", "col", None),
        P(),
        P(),
        P(),
        P(),
        P(),
        P(),
        P(),
        P(),
        P(),
    )
    return jax.shard_map(
        shards,
        mesh=mesh,
        in_specs=placed,
        out_specs=(P("row", "col", None), P("row", "col", None)),
        check_vma=False,
    )
```

profile of v0, /device:TPU:0, one launch (start us, length us, event | category | flops | bytes accessed | tf_op | source)
XLA Modules:
  0.0 554.7 jit_solution(972236072395999321)
XLA Ops:
  16.7 43.4 %all-gather.9.cloned.1.call-done = bf16[811008]{0:T(1024)(128)(2,1)} async-done(((bf16[101376]{0:T(1024)(128)(2,1)}), bf16[811008]{0:T(1024)(128)(2,1)}) %all-gather.9.cloned.1.call-update) | async-done | bytes 1622032 | tf_op jit(solution)/shard_map/all_gather | solution.py:18
  89.2 25.7 %all-to-all-done.1 = bf16[32,16,1536]{2,0,1:T(8,128)(2,1)} async-done(((bf16[32,16,1536]{2,0,1:T(8,128)(2,1)}), bf16[32,16,1536]{2,0,1:T(8,128)(2,1)}, u32[]{:S(2)}, u32[]{:S(2)}) %all-to-all-start.1) | async-done | bytes 1572896 | tf_op jit(solution)/shard_map/all_to_all | solution.py:158
  114.9 13.3 %all-gather.5.cloned.1.call-done = bf16[512,3168]{1,0:T(8,128)(2,1)} async-done(((bf16[32,3168]{1,0:T(8,128)(2,1)}), bf16[512,3168]{1,0:T(8,128)(2,1)}) %all-gather.5.cloned.1.call-update) | async-done | bytes 3244048 | tf_op jit(solution)/shard_map/all_gather | solution.py:32
  128.2 9.5 %convolution_convert_fusion = bf16[1536,3072]{1,0:T(8,128)(2,1)} fusion(bf16[512,1536]{1,0:T(8,128)(2,1)} %bitcast.18, bf16[512,3168]{1,0:T(8,128)(2,1)} %all-gather.5.cloned.1.call-done), kind=kOutput, calls=%fused_computation.13 | convolution fusion | flops 4836556800 | bytes 14155776 | tf_op jit(solution)/shard_map/dot_general | solution.py:162
  137.7 41.0 %reshape.210 = bf16[48,32,96,32]{3,2,1,0:T(8,128)(2,1)} reshape(bf16[1536,3072]{1,0:T(8,128)(2,1)} %convolution_convert_fusion) | data formatting | bytes 18874368 | tf_op jit(solution)/shard_map/reshape | solution.py:168
  179.8 17.1 %fusion.31 = (f32[48,96]{1,0:T(8,128)S(1)}, f32[48,96,128]{2,1,0:T(8,128)S(1)}) fusion(f32[48,96,128]{2,1,0:T(8,128)} %param.18, f32[48,96]{1,0:T(8,128)S(1)} %broadcast_multiply_fusion.1, f32[48,96]{1,0:T(8,128)S(1)} %convolution_add_fusion, bf16[48,32,96,32]{3,2,1,0:T(8,128)(2,1)} %reshape.210, bf16[32,32,128,1]{2,1,0,3:T(8,128)(2,1)S(1)} %bitcast.115), kind=kOutput, calls=%fused_computation.62 | convolution fusion | flops 1210314240 | bytes 14473216 | tf_op jit(solution)/shard_map/iajb,abk->ijk/dot_general | solution.py:172
  200.8 16.6 %all_to_all.79 = bf16[8,8,48,96]{3,2,1,0:T(8,128)(2,1)S(1)} all-to-all(bf16[8,8,48,96]{3,2,1,0:T(8,128)(2,1)S(1)} %broadcast_in_dim.6), channel_id=1, replica_groups=mesh['row'=16,'col'=8] {'col'}, dimensions={0} | all-to-all | bytes 1179648 | tf_op jit(solution)/shard_map/all_to_all | solution.py:37
  231.5 30.3 %all-to-all-done = bf16[32,96,257]{1,2,0:T(8,128)(2,1)} async-done(((bf16[32,96,257]{1,2,0:T(8,128)(2,1)}), bf16[32,96,257]{1,2,0:T(8,128)(2,1)}, u32[]{:S(2)}, u32[]{:S(2)}) %all-to-all-start) | async-done | bytes 1579040 | tf_op jit(solution)/shard_map/all_to_all | solution.py:48
  273.7 41.4 %all-gather.7.cloned.1.call-done = bf16[8,768,768]{2,0,1:T(8,128)(2,1)} async-done(((bf16[8,48,768]{2,0,1:T(8,128)(2,1)}), bf16[8,768,768]{2,0,1:T(8,128)(2,1)}) %all-gather.7.cloned.1.call-update) | async-done | bytes 9437200 | tf_op jit(solution)/shard_map/all_gather | solution.py:197
  315.1 15.4 %copy.95 = f32[8,768,768]{1,2,0:T(8,128)} copy(bf16[8,768,768]{2,0,1:T(8,128)(2,1)} %all-gather.7.cloned.1.call-done) | data formatting | bytes 28311552 | tf_op jit(solution)/shard_map/while | solution.py:111
  330.5 186.1 %while.12 = (s32[]{:T(128)}, bf16[4,1,768,256]{2,3,1,0:T(8,128)(2,1)}, bf16[4,1,768,256]{3,2,0,1:T(8,128)(2,1)}, bf16[4,1,768,256]{3,2,0,1:T(8,128)(2,1)}, bf16[...) while((s32[]{:T(128)}, ...), condition=%wide.region_7.8_spmd, body=%wide.region_4.7_spmd.sunk | while | flops 642918144 | bytes 85385320 | solution.py:111
  333.2 12.1 %add_add_fusion.2 = f32[8,768,768]{1,2,0:T(8,128)} fusion(f32[8,768,768]{1,2,0:T(8,128)} %get-tuple-element.252, f32[768]{0:T(1024)S(1)} %multiply_reduce_fusion.3, bf16[768,8,32]{0,2,1:T(8,128)(2,1)S(1)} %bitcast.100, bf16[768,8,32]{0,2,1:T(8,128)(2,1)S(1)} %bitcast.101), kind=kOutput, calls=%fused_computation.3.clone.1 | convolution fusion | flops 316145664 | bytes 38538240 | tf_op jit(solution)/shard_map/while/body/eval_jaxpr/bqhd,bkhd->bhqk/dot_general | solution.py:91
  345.3 13.7 %fusion.55 = f32[8,768]{1,0:T(8,128)S(1)} fusion(f32[8,768,768]{1,2,0:T(8,128)} %add_add_fusion.2), kind=kOutput, calls=%fused_computation.60.clone.1 | output fusion | flops 9437951 | bytes 18898944 | tf_op jit(solution)/shard_map/while/body/eval_jaxpr/sub | solution.py:100
  359.2 16.6 %fusion.56 = f32[8,32,768]{2,1,0:T(8,128)S(1)} fusion(bf16[768,8,32]{0,2,1:T(8,128)(2,1)S(1)} %bitcast.103, f32[8,768]{1,0:T(8,128)S(1)} %fusion.55, f32[8,768,768]{1,2,0:T(8,128)} %add_add_fusion.2), kind=kOutput, calls=%fused_computation.4.clone.1 | convolution fusion | flops 316152576 | bytes 20078592 | tf_op jit(solution)/shard_map/while/body/eval_jaxpr/bhqk,bkhd->bqhd/dot_general | solution.py:102
  379.8 12.1 %add_add_fusion.2 = f32[8,768,768]{1,2,0:T(8,128)} fusion(f32[8,768,768]{1,2,0:T(8,128)} %get-tuple-element.252, f32[768]{0:T(1024)S(1)} %multiply_reduce_fusion.3, bf16[768,8,32]{0,2,1:T(8,128)(2,1)S(1)} %bitcast.100, bf16[768,8,32]{0,2,1:T(8,128)(2,1)S(1)} %bitcast.101), kind=kOutput, calls=%fused_computation.3.clone.1 | convolution fusion | flops 316145664 | bytes 38538240 | tf_op jit(solution)/shard_map/while/body/eval_jaxpr/bqhd,bkhd->bhqk/dot_general | solution.py:91
  391.9 13.7 %fusion.55 = f32[8,768]{1,0:T(8,128)S(1)} fusion(f32[8,768,768]{1,2,0:T(8,128)} %add_add_fusion.2), kind=kOutput, calls=%fused_computation.60.clone.1 | output fusion | flops 9437951 | bytes 18898944 | tf_op jit(solution)/shard_map/while/body/eval_jaxpr/sub | solution.py:100
  405.8 16.6 %fusion.56 = f32[8,32,768]{2,1,0:T(8,128)S(1)} fusion(bf16[768,8,32]{0,2,1:T(8,128)(2,1)S(1)} %bitcast.103, f32[8,768]{1,0:T(8,128)S(1)} %fusion.55, f32[8,768,768]{1,2,0:T(8,128)} %add_add_fusion.2), kind=kOutput, calls=%fused_computation.4.clone.1 | convolution fusion | flops 316152576 | bytes 20078592 | tf_op jit(solution)/shard_map/while/body/eval_jaxpr/bhqk,bkhd->bqhd/dot_general | solution.py:102
  426.3 12.1 %add_add_fusion.2 = f32[8,768,768]{1,2,0:T(8,128)} fusion(f32[8,768,768]{1,2,0:T(8,128)} %get-tuple-element.252, f32[768]{0:T(1024)S(1)} %multiply_reduce_fusion.3, bf16[768,8,32]{0,2,1:T(8,128)(2,1)S(1)} %bitcast.100, bf16[768,8,32]{0,2,1:T(8,128)(2,1)S(1)} %bitcast.101), kind=kOutput, calls=%fused_computation.3.clone.1 | convolution fusion | flops 316145664 | bytes 38538240 | tf_op jit(solution)/shard_map/while/body/eval_jaxpr/bqhd,bkhd->bhqk/dot_general | solution.py:91
  438.4 13.7 %fusion.55 = f32[8,768]{1,0:T(8,128)S(1)} fusion(f32[8,768,768]{1,2,0:T(8,128)} %add_add_fusion.2), kind=kOutput, calls=%fused_computation.60.clone.1 | output fusion | flops 9437951 | bytes 18898944 | tf_op jit(solution)/shard_map/while/body/eval_jaxpr/sub | solution.py:100
  452.3 16.6 %fusion.56 = f32[8,32,768]{2,1,0:T(8,128)S(1)} fusion(bf16[768,8,32]{0,2,1:T(8,128)(2,1)S(1)} %bitcast.103, f32[8,768]{1,0:T(8,128)S(1)} %fusion.55, f32[8,768,768]{1,2,0:T(8,128)} %add_add_fusion.2), kind=kOutput, calls=%fused_computation.4.clone.1 | convolution fusion | flops 316152576 | bytes 20078592 | tf_op jit(solution)/shard_map/while/body/eval_jaxpr/bhqk,bkhd->bqhd/dot_general | solution.py:102
  472.8 12.1 %add_add_fusion.2 = f32[8,768,768]{1,2,0:T(8,128)} fusion(f32[8,768,768]{1,2,0:T(8,128)} %get-tuple-element.252, f32[768]{0:T(1024)S(1)} %multiply_reduce_fusion.3, bf16[768,8,32]{0,2,1:T(8,128)(2,1)S(1)} %bitcast.100, bf16[768,8,32]{0,2,1:T(8,128)(2,1)S(1)} %bitcast.101), kind=kOutput, calls=%fused_computation.3.clone.1 | convolution fusion | flops 316145664 | bytes 38538240 | tf_op jit(solution)/shard_map/while/body/eval_jaxpr/bqhd,bkhd->bhqk/dot_general | solution.py:91
  484.9 13.7 %fusion.55 = f32[8,768]{1,0:T(8,128)S(1)} fusion(f32[8,768,768]{1,2,0:T(8,128)} %add_add_fusion.2), kind=kOutput, calls=%fused_computation.60.clone.1 | output fusion | flops 9437951 | bytes 18898944 | tf_op jit(solution)/shard_map/while/body/eval_jaxpr/sub | solution.py:100
  498.8 16.6 %fusion.56 = f32[8,32,768]{2,1,0:T(8,128)S(1)} fusion(bf16[768,8,32]{0,2,1:T(8,128)(2,1)S(1)} %bitcast.103, f32[8,768]{1,0:T(8,128)S(1)} %fusion.55, f32[8,768,768]{1,2,0:T(8,128)} %add_add_fusion.2), kind=kOutput, calls=%fused_computation.4.clone.1 | convolution fusion | flops 316152576 | bytes 20078592 | tf_op jit(solution)/shard_map/while/body/eval_jaxpr/bhqk,bkhd->bqhd/dot_general | solution.py:102
  519.3 25.5 %all_to_all.80 = bf16[4,768,256]{2,0,1:T(4,128)(2,1)S(1)} all-to-all(bf16[4,768,256]{2,0,1:T(4,128)(2,1)S(1)} %bitcast.107), channel_id=1, replica_groups=mesh['row'=16,'col'=8] {'col'}, dimensions={1} | all-to-all | bytes 3145728 | tf_op jit(solution)/shard_map/all_to_all | solution.py:210
  (124 shorter events, 91.4 us)
Async XLA Ops:
  7.2 260.4 %copy-start = (bf16[256,1024]{1,0:T(8,128)(2,1)S(1)}, bf16[256,1024]{1,0:T(8,128)(2,1)}, u32[]{:S(2)}) copy-start(bf16[256,1024]{1,0:T(8,128)(2,1)} %param.26) | copy-start | bytes 1572868
  7.2 2.3 copy-start.2
  7.2 3.3 copy-start.6
  7.2 3.3 copy-start.14
  7.2 3.3 copy-start.12
  7.2 52.8 %all-gather.9.cloned.1.call-start = ((), (), s32[]{:S(2)}) async-start(), calls=%async_computation.7 | async-start | bytes 1824768 | tf_op jit(solution)/shard_map/all_gather | solution.py:18
  10.6 2.9 copy-start.13
  13.4 114.8 %all-gather.5.cloned.1.call-start = ((), (), s32[]{:S(2)}) async-start(), calls=%async_computation.5 | async-start | bytes 3481600 | tf_op jit(solution)/shard_map/all_gather | solution.py:32
  65.3 15.9 %all-to-all-start.2 = ((bf16[16,2,768]{2,1,0:T(2,128)(2,1)}), bf16[16,2,768]{2,1,0:T(2,128)(2,1)S(1)}, u32[]{:S(2)}, u32[]{:S(2)}) async-start(bf16[16,2,768]{2,1,0:T(2,128)(2,1)} %reshape.227), calls=%async_computation.2 | async-start | bytes 98304 | tf_op jit(solution)/shard_map/all_to_all | solution.py:159
  81.1 7.6 %copy-start.7 = (s32[768]{0:T(1024)S(1)}, s32[768]{0:T(1024)}, u32[]{:S(2)}) copy-start(s32[768]{0:T(1024)} %param.17) | copy-start | bytes 9220
  81.1 33.8 %all-to-all-start.1 = ((bf16[32,16,1536]{2,0,1:T(8,128)(2,1)}), bf16[32,16,1536]{2,0,1:T(8,128)(2,1)}, u32[]{:S(2)}, u32[]{:S(2)}) async-start(bf16[32,16,1536]{2,0,1:T(8,128)(2,1)} %copy.83), calls=%async_computation.1 | async-start | bytes 3145728 | tf_op jit(solution)/shard_map/all_to_all | solution.py:158
  88.5 226.6 %all-gather.7.cloned.1.call-start = ((), (), s32[]{:S(2)}) async-start(), calls=%async_computation.6 | async-start | bytes 10027008 | tf_op jit(solution)/shard_map/all_gather | solution.py:197
  137.7 42.1 %copy-start.11 = (bf16[1024,128]{1,0:T(8,128)(2,1)S(1)}, bf16[1024,128]{1,0:T(8,128)(2,1)}, u32[]{:S(2)}) copy-start(bf16[1024,128]{1,0:T(8,128)(2,1)} %param.24) | copy-start | bytes 786436
  196.9 3.7 copy-start.4
  196.9 1.7 copy-start.8
  196.9 1.7 copy-start.10
  217.4 2.4 copy-start.9
  226.9 34.9 %all-to-all-start = ((bf16[32,96,257]{1,2,0:T(8,128)(2,1)}), bf16[32,96,257]{1,2,0:T(8,128)(2,1)}, u32[]{:S(2)}, u32[]{:S(2)}) async-start(bf16[32,96,257]{1,2,0:T(8,128)(2,1)} %copy.80), calls=%async_computation | async-start | bytes 4325376 | tf_op jit(solution)/shard_map/all_to_all | solution.py:48
  545.1 1.4 copy-start.3
  545.1 1.4 copy-start.5
  545.2 3.0 copy-start.1
Sparse Core Ops, SparseCore 0:
  13.6 46.4 all-gather.8
  62.5 65.7 all-gather.4
  219.5 95.5 all-gather.6
where the time goes:
time: 557 us; the launch traced here: 555 us
  waiting for transfers between devices  154 us (28%)
  matrix products  152 us (27%)
  local copies, waits for them, and re-layouts  106 us (19%)
  other arithmetic  68 us (12%)
  blocking collectives  42.1 us (8%)
  starting transfers between devices  18.4 us (3%)
  between operations  14.2 us (3%)
    dot_general x4, matrix products, one_block(): jnp.einsum('bhqk,bkhd->bqhd', weights, value_heads, preferred_element_typ...  66.6 us
    sub x4, other arithmetic, one_block(): exponent = jnp.exp(scores - highest)  54.9 us
    dot_general x4, matrix products, one_block(): jnp.einsum('bqhd,bkhd->bhqk', query_heads, key_heads, preferred_element_t...  48.4 us
    all_gather x1, waiting for transfers between devices, one_gather(): lines, at, outs = (lax.all_gather(line, axis), 0, [])  43.4 us
    all_gather x1, waiting for transfers between devices, shards(): bias_whole = lax.all_gather(bias_cols, 'row', axis=1, tiled=True)  41.4 us
    reshape x1, local copies, waits for them, and re-layouts, shards(): outer_sum.astype(jnp.bfloat16)  41 us
    all_to_all x1, waiting for transfers between devices, sent_together(): lax.all_to_all(both, axis, split_axis=split_dim, concat_axis=concat_dim,...  30.3 us
    all_to_all x1, waiting for transfers between devices, shards(): lax.all_to_all(left_wide, 'row', split_axis=1, concat_axis=0, tiled=True)  25.7 us
  transfers between devices with their start and end apart: 6, of which 5 were waited for; matrix products, arithmetic and copies ran while one was open for 6% of the time, Pallas kernels for 0%

commit v1 on v0

--- a/solution.py
+++ b/solution.py
@@ -194,7 +194,9 @@
     rows_input, rows_mask = sent_together(
         (exponential_probabilities, shrunk_availability), "col", 0, 1, 2
     )
-    bias_whole = lax.all_gather(bias_cols, "row", axis=1, tiled=True)
+    bias_whole = jnp.concatenate(
+        lax.all_to_all(jnp.stack([bias_cols] * lax.axis_size("row")), "row", 0, 0), axis=1
+    )
     projected = jnp.einsum(
         "src,cd->srd", rows_input, asker_lookup_sigmoid_kernel, preferred_element_type=jnp.float32
     ).astype(jnp.bfloat16)

time: 557 us -> 675 us (1.21)
  waiting for transfers between devices: 154 us -> 259 us
  blocking collectives: 42.1 us -> 23 us
  other arithmetic: 68 us -> 80.8 us
  starting transfers between devices: 18.4 us -> 26.5 us
  local copies, waits for them, and re-layouts: 106 us -> 114 us
    all_to_all x0 -> x2, waiting for transfers between devices: none -> 148 us  [the longest x1 140 us: shards(): lax.all_to_all(jnp.stack([bias_cols] * lax.axis_size('row')), 'row', 0, 0)]
    all_gather x1 -> x0, waiting for transfers between devices: 41.4 us -> none  [shards(): bias_whole = lax.all_gather(bias_cols, 'row', axis=1, tiled=True)]
    all_to_all x1 -> x0, blocking collectives: 16.6 us -> none  [sent_to_all(): return lax.all_to_all(copies, axis, split_axis=0, concat_axis=0, tiled=True)]
    convert_element_type x0 -> x1, other arithmetic: none -> 12.8 us  [attend(): bias_float = bias_rows.astype(jnp.float32)]
    all_to_all x0 -> x2, starting transfers between devices: none -> 9.22 us  [the longest x1 5.01 us: shards(): lax.all_to_all(jnp.stack([bias_cols] * lax.axis_size('row')), 'row', 0, 0)]
    another operation x0 -> x2, local copies, waits for them, and re-layouts: none -> 7.49 us  [shards(): jnp.stack([bias_cols] * lax.axis_size('row'))]
  transfers between devices with their start and end apart: 6 -> 7, of which waited for: 5 -> 6; matrix products, arithmetic and copies ran while one was open for 6% -> 5% of each run, Pallas kernels for 0% -> 0%
where the time goes in v1:
time: 675 us; the launch traced here: 670 us
  waiting for transfers between devices  259 us (38%)
  matrix products  152 us (23%)
  local copies, waits for them, and re-layouts  114 us (17%)
  other arithmetic  80.8 us (12%)
  starting transfers between devices  26.5 us (4%)
  blocking collectives  23 us (3%)
  between operations  14.5 us (2%)
    all_to_all x1, waiting for transfers between devices, shards(): lax.all_to_all(jnp.stack([bias_cols] * lax.axis_size('row')), 'row', 0, 0)  140 us
    dot_general x4, matrix products, one_block(): jnp.einsum('bhqk,bkhd->bqhd', weights, value_heads, preferred_element_typ...  66.6 us
    sub x4, other arithmetic, one_block(): exponent = jnp.exp(scores - highest)  54.9 us
    dot_general x4, matrix products, one_block(): jnp.einsum('bqhd,bkhd->bhqk', query_heads, key_heads, preferred_element_t...  48.6 us
    all_gather x1, waiting for transfers between devices, one_gather(): lines, at, outs = (lax.all_gather(line, axis), 0, [])  43.3 us
    reshape x1, local copies, waits for them, and re-layouts, shards(): outer_sum.astype(jnp.bfloat16)  41 us
    all_to_all x1, waiting for transfers between devices, sent_together(): lax.all_to_all(both, axis, split_axis=split_dim, concat_axis=concat_dim,...  28.7 us
    all_to_all x1, waiting for transfers between devices, shards(): lax.all_to_all(left_wide, 'row', split_axis=1, concat_axis=0, tiled=True)  25.9 us
  transfers between devices with their start and end apart: 7, of which 6 were waited for; matrix products, arithmetic and copies ran while one was open for 5% of the time, Pallas kernels for 0%

profile of v1, /device:TPU:0, one launch (start us, length us, event | category | flops | bytes accessed | tf_op | source)
XLA Modules:
  0.0 670.1 jit_solution(11215026353240403487)
XLA Ops:
  16.7 43.3 %all-gather.6.cloned.1.call-done = bf16[811008]{0:T(1024)(128)(2,1)} async-done(((bf16[101376]{0:T(1024)(128)(2,1)}), bf16[811008]{0:T(1024)(128)(2,1)}) %all-gather.6.cloned.1.call-update) | async-done | bytes 1622032 | tf_op jit(solution)/shard_map/all_gather | solution.py:18
  89.0 25.9 %all-to-all-done.1 = bf16[32,16,1536]{2,0,1:T(8,128)(2,1)} async-done(((bf16[32,16,1536]{2,0,1:T(8,128)(2,1)}), bf16[32,16,1536]{2,0,1:T(8,128)(2,1)}, u32[]{:S(2)}, u32[]{:S(2)}) %all-to-all-start.1) | async-done | bytes 1572896 | tf_op jit(solution)/shard_map/all_to_all | solution.py:158
  114.9 13.3 %all-gather.4.cloned.1.call-done = bf16[512,3168]{1,0:T(8,128)(2,1)} async-done(((bf16[32,3168]{1,0:T(8,128)(2,1)}), bf16[512,3168]{1,0:T(8,128)(2,1)}) %all-gather.4.cloned.1.call-update) | async-done | bytes 3244048 | tf_op jit(solution)/shard_map/all_gather | solution.py:32
  128.2 9.5 %convolution_convert_fusion = bf16[1536,3072]{1,0:T(8,128)(2,1)} fusion(bf16[512,1536]{1,0:T(8,128)(2,1)} %bitcast.18, bf16[512,3168]{1,0:T(8,128)(2,1)} %all-gather.4.cloned.1.call-done), kind=kOutput, calls=%fused_computation.13 | convolution fusion | flops 4836556800 | bytes 14155776 | tf_op jit(solution)/shard_map/dot_general | solution.py:162
  137.7 41.0 %reshape.213 = bf16[48,32,96,32]{3,2,1,0:T(8,128)(2,1)} reshape(bf16[1536,3072]{1,0:T(8,128)(2,1)} %convolution_convert_fusion) | data formatting | bytes 18874368 | tf_op jit(solution)/shard_map/reshape | solution.py:168
  179.8 18.3 %fusion.31 = (f32[48,96]{1,0:T(8,128)S(1)}, f32[48,96,128]{2,1,0:T(8,128)}) fusion(f32[48,96,128]{2,1,0:T(8,128)} %param.18, f32[48,96]{1,0:T(8,128)S(1)} %broadcast_multiply_fusion.1, f32[48,96]{1,0:T(8,128)S(1)} %convolution_add_fusion, bf16[48,32,96,32]{3,2,1,0:T(8,128)(2,1)} %reshape.213, bf16[32,32,128,1]{2,1,0,3:T(8,128)(2,1)S(1)} %bitcast.117), kind=kOutput, calls=%fused_computation.63 | convolution fusion | flops 1210314240 | bytes 14473216 | tf_op jit(solution)/shard_map/iajb,abk->ijk/dot_general | solution.py:172
  228.7 28.7 %all-to-all-done = bf16[32,96,257]{1,2,0:T(8,128)(2,1)S(1)} async-done(((bf16[32,96,257]{1,2,0:T(8,128)(2,1)}), bf16[32,96,257]{1,2,0:T(8,128)(2,1)S(1)}, u32[]{:S(2)}, u32[]{:S(2)}) %all-to-all-start) | async-done | bytes 1579040 | tf_op jit(solution)/shard_map/all_to_all | solution.py:48
  276.6 139.8 %all-to-all-done.4 = bf16[16,8,48,768]{3,2,1,0:T(8,128)(2,1)} async-done(((bf16[16,8,48,768]{3,2,1,0:T(8,128)(2,1)}), bf16[16,8,48,768]{3,2,1,0:T(8,128)(2,1)}, u32[]{:S(2)}, u32[]{:S(2)}) %all-to-all-start.4) | async-done | bytes 9437216 | tf_op jit(solution)/shard_map/all_to_all | solution.py:198
  416.4 12.8 %copy_convert_fusion = f32[16,8,48,768]{3,2,0,1:T(8,128)} fusion(bf16[16,8,48,768]{3,2,1,0:T(8,128)(2,1)} %all-to-all-done.4), kind=kLoop, calls=%fused_computation.14 | loop fusion | flops 4718592 | bytes 28311552 | tf_op jit(solution)/shard_map/convert_element_type | solution.py:84
  429.2 18.7 %copy.98 = f32[8,768,768]{1,2,0:T(8,128)} copy(f32[8,768,768]{2,1,0:T(8,128)} %bitcast.101) | data formatting | bytes 37748736 | tf_op jit(solution)/shard_map/while | solution.py:111
  447.8 186.3 %while.12 = (s32[]{:T(128)}, bf16[4,1,768,256]{2,3,1,0:T(8,128)(2,1)}, bf16[4,1,768,256]{3,2,0,1:T(8,128)(2,1)}, bf16[4,1,768,256]{3,2,0,1:T(8,128)(2,1)}, bf16[...) while((s32[]{:T(128)}, ...), condition=%wide.region_7.8_spmd, body=%wide.region_4.7_spmd.sunk | while | flops 642918144 | bytes 85385320 | solution.py:111
  450.6 12.1 %add_add_fusion.2 = f32[8,768,768]{1,2,0:T(8,128)} fusion(f32[8,768,768]{1,2,0:T(8,128)} %get-tuple-element.252, f32[768]{0:T(1024)S(1)} %multiply_reduce_fusion.3, bf16[768,8,32]{0,2,1:T(8,128)(2,1)S(1)} %bitcast.102, bf16[768,8,32]{0,2,1:T(8,128)(2,1)S(1)} %bitcast.103), kind=kOutput, calls=%fused_computation.3.clone.1 | convolution fusion | flops 316145664 | bytes 38538240 | tf_op jit(solution)/shard_map/while/body/eval_jaxpr/bqhd,bkhd->bhqk/dot_general | solution.py:91
  462.7 13.7 %fusion.55 = f32[8,768]{1,0:T(8,128)S(1)} fusion(f32[8,768,768]{1,2,0:T(8,128)} %add_add_fusion.2), kind=kOutput, calls=%fused_computation.61.clone.1 | output fusion | flops 9437951 | bytes 18898944 | tf_op jit(solution)/shard_map/while/body/eval_jaxpr/sub | solution.py:100
  476.6 16.6 %fusion.56 = f32[8,32,768]{2,1,0:T(8,128)S(1)} fusion(bf16[768,8,32]{0,2,1:T(8,128)(2,1)S(1)} %bitcast.105, f32[8,768]{1,0:T(8,128)S(1)} %fusion.55, f32[8,768,768]{1,2,0:T(8,128)} %add_add_fusion.2), kind=kOutput, calls=%fused_computation.4.clone.1 | convolution fusion | flops 316152576 | bytes 20078592 | tf_op jit(solution)/shard_map/while/body/eval_jaxpr/bhqk,bkhd->bqhd/dot_general | solution.py:102
  497.1 12.1 %add_add_fusion.2 = f32[8,768,768]{1,2,0:T(8,128)} fusion(f32[8,768,768]{1,2,0:T(8,128)} %get-tuple-element.252, f32[768]{0:T(1024)S(1)} %multiply_reduce_fusion.3, bf16[768,8,32]{0,2,1:T(8,128)(2,1)S(1)} %bitcast.102, bf16[768,8,32]{0,2,1:T(8,128)(2,1)S(1)} %bitcast.103), kind=kOutput, calls=%fused_computation.3.clone.1 | convolution fusion | flops 316145664 | bytes 38538240 | tf_op jit(solution)/shard_map/while/body/eval_jaxpr/bqhd,bkhd->bhqk/dot_general | solution.py:91
  509.3 13.7 %fusion.55 = f32[8,768]{1,0:T(8,128)S(1)} fusion(f32[8,768,768]{1,2,0:T(8,128)} %add_add_fusion.2), kind=kOutput, calls=%fused_computation.61.clone.1 | output fusion | flops 9437951 | bytes 18898944 | tf_op jit(solution)/shard_map/while/body/eval_jaxpr/sub | solution.py:100
  523.2 16.6 %fusion.56 = f32[8,32,768]{2,1,0:T(8,128)S(1)} fusion(bf16[768,8,32]{0,2,1:T(8,128)(2,1)S(1)} %bitcast.105, f32[8,768]{1,0:T(8,128)S(1)} %fusion.55, f32[8,768,768]{1,2,0:T(8,128)} %add_add_fusion.2), kind=kOutput, calls=%fused_computation.4.clone.1 | convolution fusion | flops 316152576 | bytes 20078592 | tf_op jit(solution)/shard_map/while/body/eval_jaxpr/bhqk,bkhd->bqhd/dot_general | solution.py:102
  543.7 12.1 %add_add_fusion.2 = f32[8,768,768]{1,2,0:T(8,128)} fusion(f32[8,768,768]{1,2,0:T(8,128)} %get-tuple-element.252, f32[768]{0:T(1024)S(1)} %multiply_reduce_fusion.3, bf16[768,8,32]{0,2,1:T(8,128)(2,1)S(1)} %bitcast.102, bf16[768,8,32]{0,2,1:T(8,128)(2,1)S(1)} %bitcast.103), kind=kOutput, calls=%fused_computation.3.clone.1 | convolution fusion | flops 316145664 | bytes 38538240 | tf_op jit(solution)/shard_map/while/body/eval_jaxpr/bqhd,bkhd->bhqk/dot_general | solution.py:91
  555.9 13.7 %fusion.55 = f32[8,768]{1,0:T(8,128)S(1)} fusion(f32[8,768,768]{1,2,0:T(8,128)} %add_add_fusion.2), kind=kOutput, calls=%fused_computation.61.clone.1 | output fusion | flops 9437951 | bytes 18898944 | tf_op jit(solution)/shard_map/while/body/eval_jaxpr/sub | solution.py:100
  569.8 16.6 %fusion.56 = f32[8,32,768]{2,1,0:T(8,128)S(1)} fusion(bf16[768,8,32]{0,2,1:T(8,128)(2,1)S(1)} %bitcast.105, f32[8,768]{1,0:T(8,128)S(1)} %fusion.55, f32[8,768,768]{1,2,0:T(8,128)} %add_add_fusion.2), kind=kOutput, calls=%fused_computation.4.clone.1 | convolution fusion | flops 316152576 | bytes 20078592 | tf_op jit(solution)/shard_map/while/body/eval_jaxpr/bhqk,bkhd->bqhd/dot_general | solution.py:102
  590.3 12.1 %add_add_fusion.2 = f32[8,768,768]{1,2,0:T(8,128)} fusion(f32[8,768,768]{1,2,0:T(8,128)} %get-tuple-element.252, f32[768]{0:T(1024)S(1)} %multiply_reduce_fusion.3, bf16[768,8,32]{0,2,1:T(8,128)(2,1)S(1)} %bitcast.102, bf16[768,8,32]{0,2,1:T(8,128)(2,1)S(1)} %bitcast.103), kind=kOutput, calls=%fused_computation.3.clone.1 | convolution fusion | flops 316145664 | bytes 38538240 | tf_op jit(solution)/shard_map/while/body/eval_jaxpr/bqhd,bkhd->bhqk/dot_general | solution.py:91
  602.5 13.7 %fusion.55 = f32[8,768]{1,0:T(8,128)S(1)} fusion(f32[8,768,768]{1,2,0:T(8,128)} %add_add_fusion.2), kind=kOutput, calls=%fused_computation.61.clone.1 | output fusion | flops 9437951 | bytes 18898944 | tf_op jit(solution)/shard_map/while/body/eval_jaxpr/sub | solution.py:100
  616.4 16.6 %fusion.56 = f32[8,32,768]{2,1,0:T(8,128)S(1)} fusion(bf16[768,8,32]{0,2,1:T(8,128)(2,1)S(1)} %bitcast.105, f32[8,768]{1,0:T(8,128)S(1)} %fusion.55, f32[8,768,768]{1,2,0:T(8,128)} %add_add_fusion.2), kind=kOutput, calls=%fused_computation.4.clone.1 | convolution fusion | flops 316152576 | bytes 20078592 | tf_op jit(solution)/shard_map/while/body/eval_jaxpr/bhqk,bkhd->bqhd/dot_general | solution.py:102
  636.9 23.0 %all_to_all.84 = bf16[4,768,256]{2,0,1:T(4,128)(2,1)S(1)} all-to-all(bf16[4,768,256]{2,0,1:T(4,128)(2,1)S(1)} %bitcast.110), channel_id=1, replica_groups=mesh['row'=16,'col'=8] {'col'}, dimensions={1} | all-to-all | bytes 3145728 | tf_op jit(solution)/shard_map/all_to_all | solution.py:212
  (130 shorter events, 111.0 us)
Async XLA Ops:
  7.2 264.7 %copy-start = (bf16[256,1024]{1,0:T(8,128)(2,1)S(1)}, bf16[256,1024]{1,0:T(8,128)(2,1)}, u32[]{:S(2)}) copy-start(bf16[256,1024]{1,0:T(8,128)(2,1)} %param.26) | copy-start | bytes 1572868
  7.2 2.3 copy-start.2
  7.2 3.3 copy-start.8
  7.2 3.3 copy-start.16
  7.2 3.3 copy-start.14
  7.2 52.8 %all-gather.6.cloned.1.call-start = ((), (), s32[]{:S(2)}) async-start(), calls=%async_computation.7 | async-start | bytes 1824768 | tf_op jit(solution)/shard_map/all_gather | solution.py:18
  10.6 2.9 copy-start.15
  13.4 114.8 %all-gather.4.cloned.1.call-start = ((), (), s32[]{:S(2)}) async-start(), calls=%async_computation.6 | async-start | bytes 3481600 | tf_op jit(solution)/shard_map/all_gather | solution.py:32
  65.2 15.9 %all-to-all-start.2 = ((bf16[16,2,768]{2,1,0:T(2,128)(2,1)}), bf16[16,2,768]{2,1,0:T(2,128)(2,1)S(1)}, u32[]{:S(2)}, u32[]{:S(2)}) async-start(bf16[16,2,768]{2,1,0:T(2,128)(2,1)} %reshape.229), calls=%async_computation.2 | async-start | bytes 98304 | tf_op jit(solution)/shard_map/all_to_all | solution.py:159
  81.1 7.4 %copy-start.9 = (s32[768]{0:T(1024)S(1)}, s32[768]{0:T(1024)}, u32[]{:S(2)}) copy-start(s32[768]{0:T(1024)} %param.17) | copy-start | bytes 9220
  81.1 33.8 %all-to-all-start.1 = ((bf16[32,16,1536]{2,0,1:T(8,128)(2,1)}), bf16[32,16,1536]{2,0,1:T(8,128)(2,1)}, u32[]{:S(2)}, u32[]{:S(2)}) async-start(bf16[32,16,1536]{2,0,1:T(8,128)(2,1)} %copy.86), calls=%async_computation.1 | async-start | bytes 3145728 | tf_op jit(solution)/shard_map/all_to_all | solution.py:158
  137.7 42.1 %copy-start.13 = (bf16[1024,128]{1,0:T(8,128)(2,1)S(1)}, bf16[1024,128]{1,0:T(8,128)(2,1)}, u32[]{:S(2)}) copy-start(bf16[1024,128]{1,0:T(8,128)(2,1)} %param.24) | copy-start | bytes 786436
  198.1 3.1 copy-start.4
  198.1 3.1 copy-start.10
  198.1 3.1 copy-start.12
  201.2 8.5 %copy-start.11 = (f32[256]{0:T(256)S(1)}, f32[256]{0:T(256)}, u32[]{:S(2)}) copy-start(f32[256]{0:T(256)} %param.20) | copy-start | bytes 3076
  204.2 17.7 %all-to-all-start.3 = ((bf16[8,8,48,96]{3,2,1,0:T(8,128)(2,1)}), bf16[8,8,48,96]{3,2,1,0:T(8,128)(2,1)}, u32[]{:S(2)}, u32[]{:S(2)}) async-start(bf16[8,8,48,96]{3,2,1,0:T(8,128)(2,1)} %broadcast_in_dim.6), calls=%async_computation.3 | async-start | bytes 1572864 | tf_op jit(solution)/shard_map/all_to_all | solution.py:37
  209.7 1.1 copy-start.6
  222.0 35.4 %all-to-all-start = ((bf16[32,96,257]{1,2,0:T(8,128)(2,1)}), bf16[32,96,257]{1,2,0:T(8,128)(2,1)S(1)}, u32[]{:S(2)}, u32[]{:S(2)}) async-start(bf16[32,96,257]{1,2,0:T(8,128)(2,1)} %copy.83), calls=%async_computation | async-start | bytes 4325376 | tf_op jit(solution)/shard_map/all_to_all | solution.py:48
  257.3 6.0 copy-start.5
  263.4 153.0 %all-to-all-start.4 = ((bf16[16,8,48,768]{3,2,1,0:T(8,128)(2,1)}), bf16[16,8,48,768]{3,2,1,0:T(8,128)(2,1)}, u32[]{:S(2)}, u32[]{:S(2)}) async-start(bf16[16,8,48,768]{3,2,1,0:T(8,128)(2,1)} %stack.3), calls=%async_computation.4 | async-start | bytes 18874368 | tf_op jit(solution)/shard_map/all_to_all | solution.py:198
  660.1 1.4 copy-start.3
  660.1 1.4 copy-start.7
  660.3 3.0 copy-start.1
Sparse Core Ops, SparseCore 0:
  13.6 46.4 all-gather.5
  62.5 65.7 all-gather.3
